TPU v7x, 128 devices: a whole 4x4x4 slice. The times are simulated.
128 devices in a mesh: dom: 64 (over x, z, y), batch: 2 (over core).
Axes of the slice: x: 4, y: 4, z: 4, core: 2. Of those that a mesh axis runs over, the one named last changes fastest.
Arguments:
- features: bfloat16 [4, 65536, 512], P('batch', 'dom'), may hold values from -6 to 6
- tile_vals: bfloat16 [2048, 128, 128], P('dom'), may hold values from -0.25 to 0.25
- tile_row: int32 [2048], P('dom'), may hold values from 0 to 7
- tile_col: int32 [2048], P('dom'), may hold values from 0 to 11
- send_next: int32 [128], P('dom'), may hold values from 0 to 7
- send_prev: int32 [128], P('dom'), may hold values from 0 to 7
- cluster: int32 [65536], P('dom'), may hold values from 0 to 1023, as said below
- cotangent: bfloat16 [4, 65536, 512], P('batch', 'dom'), may hold values from -6 to 6
- self_weight: bfloat16 [512, 512], replicated, may hold values from -0.25 to 0.25
- neighbour_weight: bfloat16 [512, 512], replicated, may hold values from -0.25 to 0.25
- w_coarse: bfloat16 [512, 512], replicated, may hold values from -0.25 to 0.25
Outputs:
- output: bfloat16 [4, 65536, 512], P('batch', 'dom')
- self_weight_gradient: float32 [512, 512], replicated
- neighbour_weight_gradient: float32 [512, 512], replicated
- grad_coarse: float32 [512, 512], replicated
Inputs may be any that keep to these rules, and one draw needn't show every extreme that they name: Within each pair of partitions 2m, 2m + 1, every cluster number names exactly two of the pair's 2 * 1024 nodes.
All inputs are finite; a program needn't handle non-finite values.
Results may differ from a plain program's by a relative error of at most 0.012.
Values may be sent and summed in bfloat16 or wider, within the bound.
A program may use at most 128 MiB of HBM per device.

v0:
```python
import math
import jax
import jax.numpy as jnp
from jax import lax
from jax.sharding import PartitionSpec as P


def shifted(x, axis, by):
    length = lax.axis_size(axis)
    pairs = [(i, i + by) for i in range(length) if 0 <= i + by < length]
    return lax.ppermute(x, axis, pairs)


def partner(value, axis, distance):
    mask = 2**distance
    pairs = [(source, source ^ mask) for source in range(lax.axis_size(axis))]
    return lax.ppermute(value, axis, pairs)


def dsilu(value):
    sig = jax.nn.sigmoid(value)
    return sig * (1.0 + value * (1.0 - sig))


def member_table(labels, count):
    return (labels[None, :] == jnp.arange(count, dtype=jnp.int32)[:, None]).astype(jnp.bfloat16)


def pooling(rows, table):
    return jnp.einsum("cn,snd->scd", table, rows, preferred_element_type=jnp.float32)


def lookup(coarse_rows, table):
    return jnp.einsum("cn,scd->snd", table, coarse_rows, preferred_element_type=jnp.float32)


def pick_blocks(labels, count, tiled):
    table = (labels[:, None] == jnp.arange(count, dtype=jnp.int32)[None, :]).astype(jnp.bfloat16)
    return jnp.einsum("tb,sbjd->stjd", table, tiled, preferred_element_type=jnp.float32).astype(
        jnp.bfloat16
    )


def local(
    features,
    tile_vals,
    tile_row,
    tile_col,
    send_next,
    send_prev,
    cluster,
    cotangent,
    self_weight,
    neighbour_weight,
    w_coarse,
):
    scen, nodes, width = features.shape
    side = tile_vals.shape[1]
    blocks = nodes // side
    tiled = features.reshape(scen, blocks, side, width)
    to_next = pick_blocks(send_next, blocks, tiled)
    to_prev = pick_blocks(send_prev, blocks, tiled)
    got_prev = shifted(to_next, "dom", 1)
    got_next = shifted(to_prev, "dom", -1)
    extended = jnp.concatenate([tiled, got_prev, got_next], axis=1)
    picked = pick_blocks(tile_col, extended.shape[1], extended)
    terms = jnp.einsum("tij,stjd->stid", tile_vals, picked, preferred_element_type=jnp.float32)
    rowhot = (tile_row[None, :] == jnp.arange(blocks, dtype=jnp.int32)[:, None]).astype(jnp.float32)
    summed = jnp.einsum("rt,stid->srid", rowhot, terms, precision=lax.Precision.HIGHEST)
    neighbour_total = summed.reshape(scen, nodes, width).astype(jnp.bfloat16)
    preactivation = jnp.einsum(
        "jkb,bt->jkt", features, self_weight, preferred_element_type=jnp.float32
    )
    preactivation = preactivation + jnp.einsum(
        "jkb,bt->jkt", neighbour_total, neighbour_weight, preferred_element_type=jnp.float32
    )
    hidden = jax.nn.silu(preactivation).astype(jnp.bfloat16)
    table = member_table(cluster, nodes)
    parity = lax.axis_index("dom") % 2
    half = nodes // 2
    own_start = parity * half

    def owned(array):
        return lax.dynamic_slice_in_dim(array, own_start, half, 1)

    partial_value = pooling(hidden, table)
    grad_partial = pooling(cotangent, table)
    partner_sums = partner(partial_value.astype(jnp.bfloat16), "dom", 0).astype(partial_value.dtype)
    coarse = (0.5 * (partial_value + partner_sums)).astype(jnp.bfloat16)
    act = jnp.einsum("skd,de->ske", coarse, w_coarse, preferred_element_type=jnp.float32)
    lifted = jax.nn.silu(act).astype(jnp.bfloat16)
    grad_lift = grad_partial + partner(grad_partial.astype(jnp.bfloat16), "dom", 0).astype(
        grad_partial.dtype
    )
    grad_act = (grad_lift * dsilu(act)).astype(jnp.bfloat16)
    term_coarse = jnp.einsum(
        "skd,ske->de", owned(coarse), owned(grad_act), preferred_element_type=jnp.float32
    )
    grad_down = jnp.einsum(
        "ske,de->skd", grad_act, w_coarse, preferred_element_type=jnp.float32
    ).astype(jnp.bfloat16)
    spread = lookup(lifted, table)
    output = (hidden.astype(jnp.float32) + spread).astype(jnp.bfloat16)
    back = lookup(grad_down, table)
    grad_hidden = cotangent.astype(jnp.float32) + 0.5 * back
    preactivation_gradient = (grad_hidden * dsilu(preactivation)).astype(jnp.bfloat16)
    self_contribution = jnp.einsum(
        "btv,btq->vq", features, preactivation_gradient, preferred_element_type=jnp.float32
    )
    neighbour_contribution = jnp.einsum(
        "btv,btq->vq", neighbour_total, preactivation_gradient, preferred_element_type=jnp.float32
    )
    totals = lax.psum((self_contribution, neighbour_contribution, term_coarse), ("dom", "batch"))
    gradient_scale = 1.0 / math.sqrt(scen * lax.axis_size("batch") * nodes * lax.axis_size("dom"))
    return (
        output,
        totals[0] * gradient_scale,
        totals[1] * gradient_scale,
        totals[2] * gradient_scale,
    )


def solution(mesh):
    in_specs = (
        P("batch", "dom", None),
        P("dom", None, None),
        P("dom"),
        P("dom"),
        P("dom"),
        P("dom"),
        P("dom"),
        P("batch", "dom", None),
        P(),
        P(),
        P(),
    )
    out_specs = (P("batch", "dom", None), P(), P(), P())
    return jax.shard_map(local, mesh=mesh, in_specs=in_specs, out_specs=out_specs, check_vma=False)
```

profile of v0, /device:TPU:1, one launch (start us, length us, event | category | flops | bytes accessed | tf_op | source)
XLA Modules:
  0.0 384.3 jit_solution(13734323582045857980)
XLA Ops:
  7.2 3.2 fusion.35
  10.5 4.1 %collective-permute-start = (bf16[2,2,128,512]{3,1,2,0:T(2,128)(2,1)S(1)}, bf16[2,2,128,512]{3,1,2,0:T(2,128)(2,1)S(1)}, u32[]{:S(2)}, u32[]{:S(2)}) collective-permute-start(bf16[2,2,128,512]{3,1,2,0:T(2,128)(2,1)S(1)} %fusion.35), channel_id=1, source_target_pairs={{0,2},{2,4},{4,6},{6,8},{8,10},{10,12},{12,14},{14,16},{16,18},{18... | collective-permute-start | bytes 1572872 | tf_op jit(solution)/shard_map/ppermute | solution.py:11
  14.5 3.1 fusion.36
  17.6 1.3 collective-permute-start.1
  18.9 1.2 copy.58
  20.1 3.3 fusion.45
  23.4 1.7 collective-permute-done
  25.1 6.9 %collective-permute-done.1 = bf16[2,2,128,512]{3,1,2,0:T(2,128)(2,1)S(1)} collective-permute-done((bf16[2,2,128,512]{3,1,2,0:T(2,128)(2,1)S(1)}, bf16[2,2,128,512]{3,1,2,0:T(2,128)(2,1)S(1)}, u32[]{:S(2)}, u32[]{:S(2)}) %collective-permute-start.1) | collective-permute-done | bytes 524320 | tf_op jit(solution)/shard_map/ppermute | solution.py:11
  32.0 5.3 %convert_bitcast_fusion = bf16[2,32,128,512]{3,1,2,0:T(8,128)(2,1)} fusion(bf16[2,2,128,512]{3,1,2,0:T(2,128)(2,1)S(1)} %collective-permute-done.1, bf16[2,2,128,512]{3,1,2,0:T(2,128)(2,1)S(1)} %collective-permute-done, bf16[2,8,128,512]{3,1,2,0:T(8,128)(2,1)S(1)} %copy.58, s32[32]{0:T(128)S(1)} %copy-done.15), kind=kOutput, calls=%fused_computation.2 | convolution fusion | flops 114295168 | bytes 11534464 | tf_op jit(solution)/shard_map/tb,sbjd->stjd/dot_general | solution.py:39
  37.3 18.5 %convolution_bitcast_fusion = f32[2,32,128,512]{2,3,0,1:T(8,128)} fusion(bf16[2,32,128,512]{3,1,2,0:T(8,128)(2,1)} %convert_bitcast_fusion, bf16[32,128,128]{2,1,0:T(8,128)(2,1)S(1)} %copy-done), kind=kOutput, calls=%fused_computation | convolution fusion | flops 1073741824 | bytes 26214400 | tf_op jit(solution)/shard_map/tij,stjd->stid/dot_general | solution.py:67
  55.8 20.1 %copy.60 = f32[2,32,128,512]{3,1,2,0:T(8,128)} copy(f32[2,32,128,512]{2,3,0,1:T(8,128)} %convolution_bitcast_fusion) | data formatting | bytes 33554432 | tf_op jit(solution)/shard_map/tij,stjd->stid/transpose | solution.py:67
  75.9 9.2 %convert_bitcast_fusion.1 = bf16[2,8,128,512]{3,1,2,0:T(8,128)(2,1)S(1)} fusion(f32[2,32,128,512]{3,1,2,0:T(8,128)} %copy.60, s32[32]{0:T(128)S(1)} %copy-done.11), kind=kOutput, calls=%fused_computation.37 | convolution fusion | flops 403702016 | bytes 18874496 | tf_op jit(solution)/shard_map/rt,stid->srid/dot_general | solution.py:69
  85.8 1.3 copy-done.4
  88.1 1.2 convolution_add_fusion
  89.3 5.5 %bitcast_convert_fusion.1 = (bf16[2,1024,512]{1,2,0:T(8,128)(2,1)}, f32[2,512,1024]{2,1,0:T(8,128)}) fusion(s32[1024]{0:T(1024)S(1)} %copy-done.14, f32[2,1024,512]{2,1,0:T(8,128)S(1)} %convolution_add_fusion), kind=kOutput, calls=%fused_computation.18 | convolution fusion | flops 2154823680 | bytes 10489856 | tf_op jit(solution)/shard_map/cn,snd->scd/dot_general | solution.py:30
  94.8 1.3 collective-permute-start.2
  96.1 5.0 %bitcast_convert_fusion = (bf16[2,1024,512]{2,1,0:T(8,128)(2,1)}, f32[1024,2,512]{2,0,1:T(8,128)}) fusion(bf16[2,1024,512]{2,1,0:T(8,128)(2,1)S(1)} %copy-done.12, s32[1024]{0:T(1024)S(1)} %copy-done.14), kind=kOutput, calls=%fused_computation.12 | convolution fusion | flops 2149580800 | bytes 8392704 | tf_op jit(solution)/shard_map/cn,snd->scd/dot_general | solution.py:30
  101.5 38.9 %collective-permute-done.2 = bf16[2,1024,512]{1,2,0:T(8,128)(2,1)} collective-permute-done((bf16[2,1024,512]{1,2,0:T(8,128)(2,1)}, bf16[2,1024,512]{1,2,0:T(8,128)(2,1)}, u32[]{:S(2)}, u32[]{:S(2)}) %collective-permute-start.2) | collective-permute-done | bytes 2097184 | tf_op jit(solution)/shard_map/ppermute | solution.py:17
  140.4 3.8 fusion.12
  144.2 41.1 %collective-permute-done.3 = bf16[2,1024,512]{2,1,0:T(8,128)(2,1)} collective-permute-done((bf16[2,1024,512]{2,1,0:T(8,128)(2,1)}, bf16[2,1024,512]{2,1,0:T(8,128)(2,1)}, u32[]{:S(2)}, u32[]{:S(2)}) %collective-permute-start.3) | collective-permute-done | bytes 2097184 | tf_op jit(solution)/shard_map/ppermute | solution.py:17
  185.3 6.8 %fusion.9 = (bf16[2,1024,512]{2,1,0:T(8,128)(2,1)}, f32[2,1024,512]{2,1,0:T(8,128)}) fusion(f32[1024,2,512]{2,0,1:T(8,128)S(1)} %copy-done.17, bf16[2,1024,512]{2,1,0:T(8,128)(2,1)} %collective-permute-done.3, bf16[2,1024,512]{1,2,0:T(8,128)(2,1)S(1)} %fusion.12, bf16[512,512]{1,0:T(8,128)(2,1)S(1)} %copy-done.13), kind=kOutput, calls=%fused_computation.14 | convolution fusion | flops 1085276160 | bytes 15204352 | tf_op jit(solution)/shard_map/skd,de->ske/dot_general | solution.py:90
  192.1 8.1 %fusion.7 = bf16[2,1024,512]{2,1,0:T(8,128)(2,1)} fusion(f32[2,1024,512]{2,1,0:T(8,128)} %copy-done.5, bf16[2,1024,512]{2,1,0:T(8,128)(2,1)} %param.18, s32[1024]{0:T(1024)S(1)} %copy-done.14, bf16[2,1024,512]{2,1,0:T(8,128)(2,1)} %get-tuple-element.27, bf16[512,512]{1,0:T(8,128)(2,1)S(1)} %copy-done.13), kind=kOutput, calls=%fused_computation.10 | convolution fusion | flops 3235905536 | bytes 11014144 | tf_op jit(solution)/shard_map/cn,scd->snd/dot_general | solution.py:34
  200.2 4.6 %convolution_bitcast_fusion.2 = f32[512,512]{0,1:T(8,128)} fusion(bf16[2,1024,512]{2,1,0:T(8,128)(2,1)} %bitcast.111, bf16[2,1024,512]{2,1,0:T(8,128)(2,1)} %fusion.7), kind=kOutput, calls=%fused_computation.40 | convolution fusion | flops 1073741824 | bytes 5242880 | tf_op jit(solution)/shard_map/btv,btq->vq/dot_general | solution.py:110
  204.8 2.2 convolution_bitcast_fusion.3
  207.0 1.7 convolution_bitcast_fusion.1
  208.8 8.0 %fusion.10 = bf16[2,1024,512]{2,1,0:T(8,128)(2,1)} fusion(s32[1024]{0:T(1024)S(1)} %copy-done.14, f32[2,1024,512]{2,1,0:T(8,128)} %get-tuple-element.28, f32[2,1024,512]{2,1,0:T(8,128)} %copy-done.5), kind=kOutput, calls=%fused_computation.16 | convolution fusion | flops 2162163712 | bytes 10489856 | tf_op jit(solution)/shard_map/cn,scd->snd/dot_general | solution.py:34
  216.8 153.4 %all-reduce.3.cloned.1.call-done = (f32[512,512]{0,1:T(8,128)}, f32[512,512]{0,1:T(8,128)}, f32[512,512]{0,1:T(8,128)}) async-done(((f32[512,512]{0,1:T(8,128)}, f32[512,512]{0,1:T(8,128)}, f32[512,512]{0,1:T(8,128)}), (f32[512,512]{0,1:T(8,128)}, f32[512,512]{0,1:T(8,128)}, f32[512,512]{0,1:T(8,128)})) %all-reduce.3.cloned.1.call-update) | async-done | bytes 3145744 | tf_op jit(solution)/shard_map/psum | solution.py:113
  370.2 1.8 broadcast_multiply_fusion
  372.0 1.3 copy.73
  373.3 1.3 copy.74
  374.6 1.3 broadcast_multiply_fusion.2
  375.9 1.3 copy.72
  (39 shorter events, 2.1 us)
Async XLA Ops:
  7.2 30.1 %copy-start = (bf16[32,128,128]{2,1,0:T(8,128)(2,1)S(1)}, bf16[32,128,128]{2,1,0:T(8,128)(2,1)}, u32[]{:S(2)}) copy-start(bf16[32,128,128]{2,1,0:T(8,128)(2,1)} %param.12) | copy-start | bytes 3145732
  7.2 11.7 %copy-start.2 = (bf16[2,1024,512]{2,1,0:T(8,128)(2,1)S(1)}, bf16[2,1024,512]{2,1,0:T(8,128)(2,1)}, u32[]{:S(2)}) copy-start(bf16[2,1024,512]{2,1,0:T(8,128)(2,1)} %param.11) | copy-start | bytes 6291460
  7.2 363.0 %all-reduce.3.cloned.1.call-start = ((), (), s32[]{:S(2)}) async-start(), calls=%async_computation | async-start | bytes 6291456 | tf_op jit(solution)/shard_map/psum | solution.py:113
  7.2 12.8 %copy-start.9 = (bf16[512,512]{1,0:T(8,128)(2,1)S(1)}, bf16[512,512]{1,0:T(8,128)(2,1)}, u32[]{:S(2)}) copy-start(bf16[512,512]{1,0:T(8,128)(2,1)} %param.19) | copy-start | bytes 1572868
  10.5 14.6 %collective-permute-start = (bf16[2,2,128,512]{3,1,2,0:T(2,128)(2,1)S(1)}, bf16[2,2,128,512]{3,1,2,0:T(2,128)(2,1)S(1)}, u32[]{:S(2)}, u32[]{:S(2)}) collective-permute-start(bf16[2,2,128,512]{3,1,2,0:T(2,128)(2,1)S(1)} %fusion.35), channel_id=1, source_target_pairs={{0,2},{2,4},{4,6},{6,8},{8,10},{10,12},{12,14},{14,16},{16,18},{18... | collective-permute-start | bytes 1572872 | tf_op jit(solution)/shard_map/ppermute | solution.py:11
  17.6 14.4 %collective-permute-start.1 = (bf16[2,2,128,512]{3,1,2,0:T(2,128)(2,1)S(1)}, bf16[2,2,128,512]{3,1,2,0:T(2,128)(2,1)S(1)}, u32[]{:S(2)}, u32[]{:S(2)}) collective-permute-start(bf16[2,2,128,512]{3,1,2,0:T(2,128)(2,1)S(1)} %fusion.36), channel_id=1, source_target_pairs={{2,0},{4,2},{6,4},{8,6},{10,8},{12,10},{14,12},{16,14},{18,16},{20... | collective-permute-start | bytes 1572872 | tf_op jit(solution)/shard_map/ppermute | solution.py:11
  20.1 11.9 %copy-start.15 = (s32[32]{0:T(128)S(1)}, s32[32]{0:T(128)}, u32[]{:S(2)}) copy-start(s32[32]{0:T(128)} %param.14) | copy-start | bytes 388
  55.8 20.1 %copy-start.11 = (s32[32]{0:T(128)S(1)}, s32[32]{0:T(128)}, u32[]{:S(2)}) copy-start(s32[32]{0:T(128)} %param.13) | copy-start | bytes 388
  75.8 11.3 %copy-start.10 = (bf16[512,512]{1,0:T(8,128)(2,1)S(1)}, bf16[512,512]{1,0:T(8,128)(2,1)}, u32[]{:S(2)}) copy-start(bf16[512,512]{1,0:T(8,128)(2,1)} %param.20) | copy-start | bytes 1572868
  85.1 2.9 copy-start.3
  85.8 1.3 copy-start.4
  88.1 1.3 copy-start.14
  89.3 5.5 %copy-start.5 = (f32[2,1024,512]{2,1,0:T(8,128)}, f32[2,1024,512]{2,1,0:T(8,128)S(1)}, u32[]{:S(2)}) copy-start(f32[2,1024,512]{2,1,0:T(8,128)S(1)} %convolution_add_fusion) | copy-start | bytes 12582916
  89.3 6.8 %copy-start.12 = (bf16[2,1024,512]{2,1,0:T(8,128)(2,1)S(1)}, bf16[2,1024,512]{2,1,0:T(8,128)(2,1)}, u32[]{:S(2)}) copy-start(bf16[2,1024,512]{2,1,0:T(8,128)(2,1)} %param.18) | copy-start | bytes 6291460
  94.8 45.6 %collective-permute-start.2 = (bf16[2,1024,512]{1,2,0:T(8,128)(2,1)}, bf16[2,1024,512]{1,2,0:T(8,128)(2,1)}, u32[]{:S(2)}, u32[]{:S(2)}) collective-permute-start(bf16[2,1024,512]{1,2,0:T(8,128)(2,1)} %get-tuple-element.23), channel_id=1, source_target_pairs={{0,2},{2,0},{4,6},{6,4},{8,10},{10,8},{12,14},{14,12},{16,18},{18,... | collective-permute-start | bytes 6291464 | tf_op jit(solution)/shard_map/ppermute | solution.py:17
  101.1 84.2 %collective-permute-start.3 = (bf16[2,1024,512]{2,1,0:T(8,128)(2,1)}, bf16[2,1024,512]{2,1,0:T(8,128)(2,1)}, u32[]{:S(2)}, u32[]{:S(2)}) collective-permute-start(bf16[2,1024,512]{2,1,0:T(8,128)(2,1)} %get-tuple-element.25), channel_id=1, source_target_pairs={{0,2},{2,0},{4,6},{6,4},{8,10},{10,8},{12,14},{14,12},{16,18},{18,... | collective-permute-start | bytes 6291464 | tf_op jit(solution)/shard_map/ppermute | solution.py:17
  140.4 44.9 %copy-start.13 = (bf16[512,512]{1,0:T(8,128)(2,1)S(1)}, bf16[512,512]{1,0:T(8,128)(2,1)}, u32[]{:S(2)}) copy-start(bf16[512,512]{1,0:T(8,128)(2,1)} %param.21) | copy-start | bytes 1572868
  140.4 44.9 %copy-start.17 = (f32[1024,2,512]{2,0,1:T(8,128)S(1)}, f32[1024,2,512]{2,0,1:T(8,128)}, u32[]{:S(2)}) copy-start(f32[1024,2,512]{2,0,1:T(8,128)} %get-tuple-element.26) | copy-start | bytes 12582916
  144.2 47.9 %copy-start.7 = (bf16[2,1024,512]{1,2,0:T(8,128)(2,1)}, bf16[2,1024,512]{1,2,0:T(8,128)(2,1)S(1)}, u32[]{:S(2)}) copy-start(bf16[2,1024,512]{1,2,0:T(8,128)(2,1)S(1)} %fusion.12) | copy-start | bytes 6291460
  200.2 4.6 %copy-start.6 = (bf16[2,1024,512]{2,1,0:T(8,128)(2,1)S(1)}, bf16[2,1024,512]{2,1,0:T(8,128)(2,1)}, u32[]{:S(2)}) copy-start(bf16[2,1024,512]{2,1,0:T(8,128)(2,1)} %fusion.7) | copy-start | bytes 6291460
  204.8 2.2 copy-start.8
  204.8 2.2 copy-start.16
  371.9 5.3 %copy-start.1 = (bf16[32,128,128]{2,1,0:T(8,128)(2,1)S(1)}, bf16[32,128,128]{2,1,0:T(8,128)(2,1)}, u32[]{:S(2)}) copy-start(bf16[32,128,128]{2,1,0:T(8,128)(2,1)} %param.12) | copy-start | bytes 3145732
Sparse Core Ops, SparseCore 0:
  208.9 161.1 all-reduce.2
where the time goes:
time: 389 us; the launch traced here: 384 us
  waiting for transfers between devices  242 us (62%)
  matrix products  85.8 us (22%)
  local copies, waits for them, and re-layouts  28.1 us (7%)
  between operations  14.5 us (4%)
  starting transfers between devices  7.05 us (2%)
  other arithmetic  6.86 us (2%)
    psum x1, waiting for transfers between devices, local(): lax.psum((self_contribution, neighbour_contribution, term_coarse), ('dom'...  153 us
    ppermute x2, waiting for transfers between devices, partner(): return lax.ppermute(value, axis, pairs)  80 us
    transpose x1, local copies, waits for them, and re-layouts, local(): jnp.einsum('tij,stjd->stid', tile_vals, picked, preferred_element_type=jn...  20.1 us
    dot_general x1, matrix products, local(): jnp.einsum('tij,stjd->stid', tile_vals, picked, preferred_element_type=jn...  18.5 us
    dot_general x2, matrix products, lookup(): jnp.einsum('cn,scd->snd', table, coarse_rows, preferred_element_type=jnp....  16.1 us
    dot_general x3, matrix products, pick_blocks(): jnp.einsum('tb,sbjd->stjd', table, tiled, preferred_element_type=jnp.floa...  11.6 us
    dot_general x2, matrix products, pooling(): jnp.einsum('cn,snd->scd', table, rows, preferred_element_type=jnp.float32)  10.5 us
    dot_general x1, matrix products, local(): jnp.einsum('rt,stid->srid', rowhot, terms, precision=lax.Precision.HIGHEST)  9.25 us
  transfers between devices with their start and end apart: 5, of which 5 were waited for; matrix products, arithmetic and copies ran while one was open for 6% of the time, Pallas kernels for 0%

commit v1 on v0

--- a/solution.py
+++ b/solution.py
@@ -110,7 +110,9 @@
     neighbour_contribution = jnp.einsum(
         "btv,btq->vq", neighbour_total, preactivation_gradient, preferred_element_type=jnp.float32
     )
-    totals = lax.psum((self_contribution, neighbour_contribution, term_coarse), ("dom", "batch"))
+    totals = lax.psum(
+        lax.psum((self_contribution, neighbour_contribution, term_coarse), "batch"), "dom"
+    )
     gradient_scale = 1.0 / math.sqrt(scen * lax.axis_size("batch") * nodes * lax.axis_size("dom"))
     return (
         output,

time: 389 us -> 408 us (1.049)
  waiting for transfers between devices: 242 us -> 259 us
    psum x1 -> x2, waiting for transfers between devices: 153 us -> 171 us  [the longest x1 134 us: local(): lax.psum(lax.psum((self_contribution, neighbour_contribution, term_coarse...]
  transfers between devices with their start and end apart: 5 -> 6, of which waited for: 5 -> 6; matrix products, arithmetic and copies ran while one was open for 6% -> 6% of each run, Pallas kernels for 0% -> 0%
where the time goes in v1:
time: 408 us; the launch traced here: 402 us
  waiting for transfers between devices  259 us (63%)
  matrix products  86 us (21%)
  local copies, waits for them, and re-layouts  28.1 us (7%)
  between operations  14.5 us (4%)
  starting transfers between devices  7.26 us (2%)
  other arithmetic  6.86 us (2%)
    psum x1, waiting for transfers between devices, local(): lax.psum(lax.psum((self_contribution, neighbour_contribution, term_coarse...  134 us
    ppermute x2, waiting for transfers between devices, partner(): return lax.ppermute(value, axis, pairs)  80.1 us
    psum x1, waiting for transfers between devices, local(): lax.psum((self_contribution, neighbour_contribution, term_coarse), 'batch')  36.8 us
    transpose x1, local copies, waits for them, and re-layouts, local(): jnp.einsum('tij,stjd->stid', tile_vals, picked, preferred_element_type=jn...  20 us
    dot_general x1, matrix products, local(): jnp.einsum('tij,stjd->stid', tile_vals, picked, preferred_element_type=jn...  18.5 us
    dot_general x2, matrix products, lookup(): jnp.einsum('cn,scd->snd', table, coarse_rows, preferred_element_type=jnp....  16.1 us
    dot_general x3, matrix products, pick_blocks(): jnp.einsum('tb,sbjd->stjd', table, tiled, preferred_element_type=jnp.floa...  11.4 us
    dot_general x2, matrix products, pooling(): jnp.einsum('cn,snd->scd', table, rows, preferred_element_type=jnp.float32)  10.5 us
  transfers between devices with their start and end apart: 6, of which 6 were waited for; matrix products, arithmetic and copies ran while one was open for 6% of the time, Pallas kernels for 0%

profile of v1, /device:TPU:1, one launch (start us, length us, event | category | flops | bytes accessed | tf_op | source)
XLA Modules:
  0.0 402.1 jit_solution(16295555400429730939)
XLA Ops:
  7.2 3.2 fusion.35
  10.5 4.1 %collective-permute-start = (bf16[2,2,128,512]{3,1,2,0:T(2,128)(2,1)S(1)}, bf16[2,2,128,512]{3,1,2,0:T(2,128)(2,1)S(1)}, u32[]{:S(2)}, u32[]{:S(2)}) collective-permute-start(bf16[2,2,128,512]{3,1,2,0:T(2,128)(2,1)S(1)} %fusion.35), channel_id=1, source_target_pairs={{0,2},{2,4},{4,6},{6,8},{8,10},{10,12},{12,14},{14,16},{16,18},{18... | collective-permute-start | bytes 1572872 | tf_op jit(solution)/shard_map/ppermute | solution.py:11
  14.5 3.1 fusion.36
  17.6 1.3 collective-permute-start.1
  20.1 3.3 fusion.45
  23.4 1.7 collective-permute-done
  25.1 6.9 %collective-permute-done.1 = bf16[2,2,128,512]{3,1,2,0:T(2,128)(2,1)S(1)} collective-permute-done((bf16[2,2,128,512]{3,1,2,0:T(2,128)(2,1)S(1)}, bf16[2,2,128,512]{3,1,2,0:T(2,128)(2,1)S(1)}, u32[]{:S(2)}, u32[]{:S(2)}) %collective-permute-start.1) | collective-permute-done | bytes 524320 | tf_op jit(solution)/shard_map/ppermute | solution.py:11
  32.0 5.1 %convert_bitcast_fusion = bf16[2,32,128,512]{3,1,2,0:T(8,128)(2,1)} fusion(bf16[2,2,128,512]{3,1,2,0:T(2,128)(2,1)S(1)} %collective-permute-done.1, bf16[2,2,128,512]{3,1,2,0:T(2,128)(2,1)S(1)} %collective-permute-done, bf16[2,8,128,512]{3,1,2,0:T(8,128)(2,1)S(1)} %copy.58, s32[32]{0:T(128)S(1)} %copy-done.15), kind=kOutput, calls=%fused_computation.2 | convolution fusion | flops 114295168 | bytes 11534464 | tf_op jit(solution)/shard_map/tb,sbjd->stjd/dot_general | solution.py:39
  37.1 18.5 %convolution_bitcast_fusion = f32[2,32,128,512]{2,3,0,1:T(8,128)} fusion(bf16[2,32,128,512]{3,1,2,0:T(8,128)(2,1)} %convert_bitcast_fusion, bf16[32,128,128]{2,1,0:T(8,128)(2,1)S(1)} %copy-done), kind=kOutput, calls=%fused_computation | convolution fusion | flops 1073741824 | bytes 26214400 | tf_op jit(solution)/shard_map/tij,stjd->stid/dot_general | solution.py:67
  55.6 20.0 %copy.60 = f32[2,32,128,512]{3,1,2,0:T(8,128)} copy(f32[2,32,128,512]{2,3,0,1:T(8,128)} %convolution_bitcast_fusion) | data formatting | bytes 33554432 | tf_op jit(solution)/shard_map/tij,stjd->stid/transpose | solution.py:67
  75.6 9.6 %convert_bitcast_fusion.1 = bf16[2,8,128,512]{3,1,2,0:T(8,128)(2,1)S(1)} fusion(f32[2,32,128,512]{3,1,2,0:T(8,128)} %copy.60, s32[32]{0:T(128)S(1)} %copy-done.11), kind=kOutput, calls=%fused_computation.37 | convolution fusion | flops 403702016 | bytes 18874496 | tf_op jit(solution)/shard_map/rt,stid->srid/dot_general | solution.py:69
  85.9 1.3 copy-done.4
  88.1 1.2 convolution_add_fusion
  89.4 5.5 %bitcast_convert_fusion.1 = (bf16[2,1024,512]{1,2,0:T(8,128)(2,1)}, f32[2,512,1024]{2,1,0:T(8,128)}) fusion(s32[1024]{0:T(1024)S(1)} %copy-done.14, f32[2,1024,512]{2,1,0:T(8,128)S(1)} %convolution_add_fusion), kind=kOutput, calls=%fused_computation.18 | convolution fusion | flops 2154823680 | bytes 10489856 | tf_op jit(solution)/shard_map/cn,snd->scd/dot_general | solution.py:30
  94.9 1.3 collective-permute-start.2
  96.1 5.0 %bitcast_convert_fusion = (bf16[2,1024,512]{2,1,0:T(8,128)(2,1)}, f32[1024,2,512]{2,0,1:T(8,128)}) fusion(bf16[2,1024,512]{2,1,0:T(8,128)(2,1)S(1)} %copy-done.12, s32[1024]{0:T(1024)S(1)} %copy-done.14), kind=kOutput, calls=%fused_computation.12 | convolution fusion | flops 2149580800 | bytes 8392704 | tf_op jit(solution)/shard_map/cn,snd->scd/dot_general | solution.py:30
  101.5 38.9 %collective-permute-done.2 = bf16[2,1024,512]{1,2,0:T(8,128)(2,1)} collective-permute-done((bf16[2,1024,512]{1,2,0:T(8,128)(2,1)}, bf16[2,1024,512]{1,2,0:T(8,128)(2,1)}, u32[]{:S(2)}, u32[]{:S(2)}) %collective-permute-start.2) | collective-permute-done | bytes 2097184 | tf_op jit(solution)/shard_map/ppermute | solution.py:17
  140.4 3.8 fusion.12
  144.2 41.1 %collective-permute-done.3 = bf16[2,1024,512]{2,1,0:T(8,128)(2,1)} collective-permute-done((bf16[2,1024,512]{2,1,0:T(8,128)(2,1)}, bf16[2,1024,512]{2,1,0:T(8,128)(2,1)}, u32[]{:S(2)}, u32[]{:S(2)}) %collective-permute-start.3) | collective-permute-done | bytes 2097184 | tf_op jit(solution)/shard_map/ppermute | solution.py:17
  185.4 6.7 %fusion.9 = (bf16[2,1024,512]{2,1,0:T(8,128)(2,1)}, f32[2,1024,512]{2,1,0:T(8,128)}) fusion(f32[1024,2,512]{2,0,1:T(8,128)S(1)} %copy-done.17, bf16[2,1024,512]{2,1,0:T(8,128)(2,1)} %collective-permute-done.3, bf16[2,1024,512]{1,2,0:T(8,128)(2,1)S(1)} %fusion.12, bf16[512,512]{1,0:T(8,128)(2,1)S(1)} %copy-done.13), kind=kOutput, calls=%fused_computation.14 | convolution fusion | flops 1085276160 | bytes 15204352 | tf_op jit(solution)/shard_map/skd,de->ske/dot_general | solution.py:90
  192.1 8.1 %fusion.7 = bf16[2,1024,512]{2,1,0:T(8,128)(2,1)} fusion(f32[2,1024,512]{2,1,0:T(8,128)} %copy-done.5, bf16[2,1024,512]{2,1,0:T(8,128)(2,1)} %param.18, s32[1024]{0:T(1024)S(1)} %copy-done.14, bf16[2,1024,512]{2,1,0:T(8,128)(2,1)} %get-tuple-element.30, bf16[512,512]{1,0:T(8,128)(2,1)S(1)} %copy-done.13), kind=kOutput, calls=%fused_computation.10 | convolution fusion | flops 3235905536 | bytes 11014144 | tf_op jit(solution)/shard_map/cn,scd->snd/dot_general | solution.py:34
  200.2 4.6 %convolution_bitcast_fusion.2 = f32[512,512]{0,1:T(8,128)} fusion(bf16[2,1024,512]{2,1,0:T(8,128)(2,1)} %bitcast.111, bf16[2,1024,512]{2,1,0:T(8,128)(2,1)} %fusion.7), kind=kOutput, calls=%fused_computation.40 | convolution fusion | flops 1073741824 | bytes 5242880 | tf_op jit(solution)/shard_map/btv,btq->vq/dot_general | solution.py:110
  204.9 2.2 convolution_bitcast_fusion.3
  207.1 1.7 convolution_bitcast_fusion.1
  209.1 36.8 %all-reduce.7.cloned.1.call-done = (f32[512,512]{0,1:T(8,128)}, f32[512,512]{0,1:T(8,128)}, f32[512,512]{0,1:T(8,128)}) async-done(((f32[512,512]{0,1:T(8,128)}, f32[512,512]{0,1:T(8,128)}, f32[512,512]{0,1:T(8,128)}), (f32[512,512]{0,1:T(8,128)}, f32[512,512]{0,1:T(8,128)}, f32[512,512]{0,1:T(8,128)})) %all-reduce.7.cloned.1.call-update) | async-done | bytes 3145744 | tf_op jit(solution)/shard_map/psum | solution.py:114
  246.0 8.0 %fusion.10 = bf16[2,1024,512]{2,1,0:T(8,128)(2,1)} fusion(s32[1024]{0:T(1024)S(1)} %copy-done.14, f32[2,1024,512]{2,1,0:T(8,128)} %get-tuple-element.31, f32[2,1024,512]{2,1,0:T(8,128)} %copy-done.5), kind=kOutput, calls=%fused_computation.16 | convolution fusion | flops 2162163712 | bytes 10489856 | tf_op jit(solution)/shard_map/cn,scd->snd/dot_general | solution.py:34
  253.9 134.0 %all-reduce.5.cloned.1.call-done = (f32[512,512]{0,1:T(8,128)}, f32[512,512]{0,1:T(8,128)}, f32[512,512]{0,1:T(8,128)}) async-done(((f32[512,512]{0,1:T(8,128)}, f32[512,512]{0,1:T(8,128)}, f32[512,512]{0,1:T(8,128)}), (f32[512,512]{0,1:T(8,128)}, f32[512,512]{0,1:T(8,128)}, f32[512,512]{0,1:T(8,128)})) %all-reduce.5.cloned.1.call-update) | async-done | bytes 3145744 | tf_op jit(solution)/shard_map/psum | solution.py:113
  387.9 1.8 broadcast_multiply_fusion
  389.7 1.3 copy.73
  391.0 1.3 copy.74
  392.4 1.3 broadcast_multiply_fusion.2
  393.7 1.3 copy.72
  (42 shorter events, 3.5 us)
Async XLA Ops:
  7.2 29.9 %copy-start = (bf16[32,128,128]{2,1,0:T(8,128)(2,1)S(1)}, bf16[32,128,128]{2,1,0:T(8,128)(2,1)}, u32[]{:S(2)}) copy-start(bf16[32,128,128]{2,1,0:T(8,128)(2,1)} %param.12) | copy-start | bytes 3145732
  7.2 11.7 %copy-start.2 = (bf16[2,1024,512]{2,1,0:T(8,128)(2,1)S(1)}, bf16[2,1024,512]{2,1,0:T(8,128)(2,1)}, u32[]{:S(2)}) copy-start(bf16[2,1024,512]{2,1,0:T(8,128)(2,1)} %param.11) | copy-start | bytes 6291460
  7.2 238.7 %all-reduce.7.cloned.1.call-start = ((), (), s32[]{:S(2)}) async-start(), calls=%async_computation.1 | async-start | bytes 6291456 | tf_op jit(solution)/shard_map/psum | solution.py:114
  7.2 12.8 %copy-start.9 = (bf16[512,512]{1,0:T(8,128)(2,1)S(1)}, bf16[512,512]{1,0:T(8,128)(2,1)}, u32[]{:S(2)}) copy-start(bf16[512,512]{1,0:T(8,128)(2,1)} %param.19) | copy-start | bytes 1572868
  10.5 14.6 %collective-permute-start = (bf16[2,2,128,512]{3,1,2,0:T(2,128)(2,1)S(1)}, bf16[2,2,128,512]{3,1,2,0:T(2,128)(2,1)S(1)}, u32[]{:S(2)}, u32[]{:S(2)}) collective-permute-start(bf16[2,2,128,512]{3,1,2,0:T(2,128)(2,1)S(1)} %fusion.35), channel_id=1, source_target_pairs={{0,2},{2,4},{4,6},{6,8},{8,10},{10,12},{12,14},{14,16},{16,18},{18... | collective-permute-start | bytes 1572872 | tf_op jit(solution)/shard_map/ppermute | solution.py:11
  17.6 14.4 %collective-permute-start.1 = (bf16[2,2,128,512]{3,1,2,0:T(2,128)(2,1)S(1)}, bf16[2,2,128,512]{3,1,2,0:T(2,128)(2,1)S(1)}, u32[]{:S(2)}, u32[]{:S(2)}) collective-permute-start(bf16[2,2,128,512]{3,1,2,0:T(2,128)(2,1)S(1)} %fusion.36), channel_id=1, source_target_pairs={{2,0},{4,2},{6,4},{8,6},{10,8},{12,10},{14,12},{16,14},{18,16},{20... | collective-permute-start | bytes 1572872 | tf_op jit(solution)/shard_map/ppermute | solution.py:11
  20.1 11.9 %copy-start.15 = (s32[32]{0:T(128)S(1)}, s32[32]{0:T(128)}, u32[]{:S(2)}) copy-start(s32[32]{0:T(128)} %param.14) | copy-start | bytes 388
  55.6 20.0 %copy-start.11 = (s32[32]{0:T(128)S(1)}, s32[32]{0:T(128)}, u32[]{:S(2)}) copy-start(s32[32]{0:T(128)} %param.13) | copy-start | bytes 388
  75.6 11.6 %copy-start.10 = (bf16[512,512]{1,0:T(8,128)(2,1)S(1)}, bf16[512,512]{1,0:T(8,128)(2,1)}, u32[]{:S(2)}) copy-start(bf16[512,512]{1,0:T(8,128)(2,1)} %param.20) | copy-start | bytes 1572868
  85.2 2.9 copy-start.3
  85.9 1.3 copy-start.4
  88.1 1.3 copy-start.14
  89.4 5.5 %copy-start.5 = (f32[2,1024,512]{2,1,0:T(8,128)}, f32[2,1024,512]{2,1,0:T(8,128)S(1)}, u32[]{:S(2)}) copy-start(f32[2,1024,512]{2,1,0:T(8,128)S(1)} %convolution_add_fusion) | copy-start | bytes 12582916
  89.4 6.7 %copy-start.12 = (bf16[2,1024,512]{2,1,0:T(8,128)(2,1)S(1)}, bf16[2,1024,512]{2,1,0:T(8,128)(2,1)}, u32[]{:S(2)}) copy-start(bf16[2,1024,512]{2,1,0:T(8,128)(2,1)} %param.18) | copy-start | bytes 6291460
  94.9 45.6 %collective-permute-start.2 = (bf16[2,1024,512]{1,2,0:T(8,128)(2,1)}, bf16[2,1024,512]{1,2,0:T(8,128)(2,1)}, u32[]{:S(2)}, u32[]{:S(2)}) collective-permute-start(bf16[2,1024,512]{1,2,0:T(8,128)(2,1)} %get-tuple-element.26), channel_id=1, source_target_pairs={{0,2},{2,0},{4,6},{6,4},{8,10},{10,8},{12,14},{14,12},{16,18},{18,... | collective-permute-start | bytes 6291464 | tf_op jit(solution)/shard_map/ppermute | solution.py:17
  101.2 84.2 %collective-permute-start.3 = (bf16[2,1024,512]{2,1,0:T(8,128)(2,1)}, bf16[2,1024,512]{2,1,0:T(8,128)(2,1)}, u32[]{:S(2)}, u32[]{:S(2)}) collective-permute-start(bf16[2,1024,512]{2,1,0:T(8,128)(2,1)} %get-tuple-element.28), channel_id=1, source_target_pairs={{0,2},{2,0},{4,6},{6,4},{8,10},{10,8},{12,14},{14,12},{16,18},{18,... | collective-permute-start | bytes 6291464 | tf_op jit(solution)/shard_map/ppermute | solution.py:17
  140.4 44.9 %copy-start.13 = (bf16[512,512]{1,0:T(8,128)(2,1)S(1)}, bf16[512,512]{1,0:T(8,128)(2,1)}, u32[]{:S(2)}) copy-start(bf16[512,512]{1,0:T(8,128)(2,1)} %param.21) | copy-start | bytes 1572868
  140.4 44.9 %copy-start.17 = (f32[1024,2,512]{2,0,1:T(8,128)S(1)}, f32[1024,2,512]{2,0,1:T(8,128)}, u32[]{:S(2)}) copy-start(f32[1024,2,512]{2,0,1:T(8,128)} %get-tuple-element.29) | copy-start | bytes 12582916
  144.2 47.9 %copy-start.7 = (bf16[2,1024,512]{1,2,0:T(8,128)(2,1)}, bf16[2,1024,512]{1,2,0:T(8,128)(2,1)S(1)}, u32[]{:S(2)}) copy-start(bf16[2,1024,512]{1,2,0:T(8,128)(2,1)S(1)} %fusion.12) | copy-start | bytes 6291460
  200.2 4.6 %copy-start.6 = (bf16[2,1024,512]{2,1,0:T(8,128)(2,1)S(1)}, bf16[2,1024,512]{2,1,0:T(8,128)(2,1)}, u32[]{:S(2)}) copy-start(bf16[2,1024,512]{2,1,0:T(8,128)(2,1)} %fusion.7) | copy-start | bytes 6291460
  204.9 2.3 copy-start.8
  204.9 2.3 copy-start.16
  208.9 179.1 %all-reduce.5.cloned.1.call-start = ((), (), s32[]{:S(2)}) async-start(), calls=%async_computation | async-start | bytes 6291456 | tf_op jit(solution)/shard_map/psum | solution.py:113
  389.7 5.3 %copy-start.1 = (bf16[32,128,128]{2,1,0:T(8,128)(2,1)S(1)}, bf16[32,128,128]{2,1,0:T(8,128)(2,1)}, u32[]{:S(2)}) copy-start(bf16[32,128,128]{2,1,0:T(8,128)(2,1)} %param.12) | copy-start | bytes 3145732
Sparse Core Ops, SparseCore 0:
  209.0 36.8 all-reduce.6
  251.9 135.9 all-reduce.4
